TPU v7x, 512 devices: a whole 4x4x16 slice. The times are simulated.
512 devices in a mesh: seq: 32 (over z, core), dp: 16 (over x, y).
Axes of the slice: x: 4, y: 4, z: 16, core: 2. Of those that a mesh axis runs over, the one named last changes fastest.
Arguments:
- queries: bfloat16 [16, 5120, 2048], P('dp', 'seq'), may hold values from -6 to 6
- keys: bfloat16 [16, 5120, 2048], P('dp', 'seq'), may hold values from -6 to 6
- values: bfloat16 [16, 5120, 2048], P('dp', 'seq'), may hold values from -6 to 6
- keep: int32 [16, 5120, 2048], P('dp', 'seq'), may hold values 0 or 1
- gain: float32 [2048], replicated, may hold values from 0.25 to 1.75
- out_weight: bfloat16 [2048, 2048], P(None, 'dp'), may hold values from -0.125 to 0.125
Outputs:
- projected: bfloat16 [16, 5120, 2048], P('dp', 'seq')
All inputs are finite; a program needn't handle non-finite values. No bound on the sum of `keep` on one device may be relied on, other than what follows from the above.
Results may differ from a plain program's by a relative error of at most 0.0051.
Values may be sent and summed in bfloat16 or wider, within the bound.
No kernel may reach another device: no remote copies, remote signals or barrier semaphores. Data moves between devices by JAX's collectives and lax.ppermute only.
A program may use at most 128 MiB of HBM per device.

v0:
```python
import jax
import jax.numpy as jnp
from jax import lax
from jax.sharding import PartitionSpec as P

HEADS = 16
HEAD = 128


def prefix_2(x, axis, combine, identity):
    size, place = (lax.axis_size(axis), lax.axis_index(axis))
    everything = lax.all_gather(x, axis)
    start = jnp.broadcast_to(jnp.asarray(identity, x.dtype), x.shape)

    def turn(k, before):
        reached = k < place
        new = combine(before, everything[k])
        return jnp.where(reached, new, before)

    return lax.fori_loop(0, size, turn, start)


def feature(x):
    xf = x.astype(jnp.float32)
    return jnp.where(xf > 0, xf + 1.0, jnp.exp(jnp.minimum(xf, 0.0))).astype(jnp.bfloat16)


def add_states(earlier, later):
    return earlier + later


def on_device(queries, keys, values, keep, gain, out_weight):
    tok_rows = queries.shape[1]
    fq = feature(queries[0]).reshape(tok_rows, HEADS, HEAD)
    fk = feature(keys[0]).reshape(tok_rows, HEADS, HEAD)
    vals = values[0].reshape(tok_rows, HEADS, HEAD)
    state = jnp.einsum("thc,thd->hcd", fk, vals, preferred_element_type=jnp.float32)
    prefix = prefix_2(state, "seq", add_states, jnp.zeros_like(state))
    prefix = prefix.astype(jnp.bfloat16)
    inter = jnp.einsum("thc,hcd->thd", fq, prefix, preferred_element_type=jnp.float32)
    causal = jnp.arange(tok_rows)[:, None] >= jnp.arange(tok_rows)[None, :]
    scores = jnp.einsum("thc,shc->hts", fq, fk, preferred_element_type=jnp.float32)
    scores = jnp.where(causal[None], scores, 0.0).astype(jnp.bfloat16)
    intra = jnp.einsum("hts,shd->thd", scores, vals, preferred_element_type=jnp.float32)
    numer = inter + intra
    normed = (
        numer
        * lax.rsqrt(jnp.mean(numer * numer, axis=-1, keepdims=True) + 1e-06)
        * gain.reshape(HEADS, HEAD)
    )
    mask = keep[0].reshape(tok_rows, HEADS, HEAD).astype(jnp.float32)
    dropped = (normed * mask * (1.0 / 0.9)).astype(jnp.bfloat16).reshape(tok_rows, HEADS * HEAD)
    result = jnp.dot(
        dropped,
        lax.all_gather(out_weight, "dp", axis=1, tiled=True),
        preferred_element_type=jnp.float32,
    ).astype(jnp.bfloat16)
    return result[None]


def solution(mesh):
    return jax.shard_map(
        on_device,
        mesh=mesh,
        in_specs=(
            P("dp", "seq", None),
            P("dp", "seq", None),
            P("dp", "seq", None),
            P("dp", "seq", None),
            P(),
            P(None, "dp"),
        ),
        out_specs=P("dp", "seq", None),
        check_vma=False,
    )
```

profile of v0, /device:TPU:2, one launch (start us, length us, event | category | flops | bytes accessed | tf_op | source)
XLA Modules:
  0.0 313.0 jit_solution(7465845264773032418)
XLA Ops:
  14.4 3.3 %fusion.3 = f32[160,16,128]{2,0,1:T(8,128)} fusion(pred[160,160]{1,0:T(8,128)(4,1)S(1)} %iota_compare_fusion, bf16[160,16,128]{2,1,0:T(8,128)(2,1)} %bitcast.42, bf16[160,16,128]{2,1,0:T(8,128)(2,1)} %bitcast.41, bf16[160,16,128]{2,1,0:T(8,128)(2,1)S(1)} %bitcast.39), kind=kOutput, calls=%fused_computation.13 | convolution fusion | flops 210534400 | bytes 3302400 | tf_op jit(solution)/shard_map/hts,shd->thd/dot_general | solution.py:44
  17.7 188.8 %all-gather.6.cloned.1.call-done = f32[512,128,128]{2,1,0:T(8,128)} async-done(((f32[16,128,128]{2,1,0:T(8,128)}), f32[512,128,128]{2,1,0:T(8,128)}) %all-gather.6.cloned.1.call-update) | async-done | bytes 33554448 | tf_op jit(solution)/shard_map/all_gather | solution.py:12
  206.5 51.9 %while.14 = (s32[]{:T(128)}, f32[16,128,128]{2,1,0:T(8,128)S(1)}, s32[]{:T(128)}, f32[32,16,128,128]{3,2,1,0:T(8,128)}, s32[]{:T(128)}, /*index=5*/s32[]{:T(128)}) while((s32[]{:T(128)}, f32[16,128,128]{2,1,0:T(8,128)S(1)}, s32[]{:T(128)}, f32[32,16,128,128]{3,2,1,0:T(8,128)}, s32[]{:T(128)}, /*index=5*/s32[]{:T(128)}) %tuple.40), condition=%wide.region_1.2_spmd.clone, body=%wide.region_0.1_spmd.clone.sunk | while | flops 786436 | bytes 3145821 | solution.py:20
  206.5 1.7 add_select_fusion.2
  208.2 1.6 add_select_fusion.2
  209.8 1.6 add_select_fusion.2
  211.4 1.6 add_select_fusion.2
  213.0 1.6 add_select_fusion.2
  214.6 1.6 add_select_fusion.2
  216.2 1.6 add_select_fusion.2
  217.8 1.6 add_select_fusion.2
  221.1 1.6 add_select_fusion.2
  222.7 1.6 add_select_fusion.2
  224.3 1.7 add_select_fusion.2
  226.0 1.6 add_select_fusion.2
  227.7 1.6 add_select_fusion.2
  229.3 1.6 add_select_fusion.2
  230.9 1.6 add_select_fusion.2
  232.5 1.6 add_select_fusion.2
  234.1 1.6 add_select_fusion.2
  235.8 1.6 add_select_fusion.2
  237.4 1.6 add_select_fusion.2
  242.2 1.6 add_select_fusion.2
  243.9 1.6 add_select_fusion.2
  245.5 1.6 add_select_fusion.2
  250.3 1.6 add_select_fusion.2
  251.9 1.6 add_select_fusion.2
  253.5 1.6 add_select_fusion.2
  256.8 1.6 add_select_fusion.2
  258.4 3.1 multiply_reduce_fusion
  261.5 38.1 %all-gather.4.cloned.1.call-done = bf16[2048,2048]{1,0:T(8,128)(2,1)} async-done(((bf16[2048,128]{1,0:T(8,128)(2,1)}), bf16[2048,2048]{1,0:T(8,128)(2,1)}) %all-gather.4.cloned.1.call-update) | async-done | bytes 8388624 | tf_op jit(solution)/shard_map/all_gather | solution.py:55
  299.6 6.6 %fusion = bf16[1,160,2048]{2,1,0:T(8,128)(2,1)} fusion(bf16[2048,2048]{1,0:T(8,128)(2,1)} %all-gather.4.cloned.1.call-done, f32[160,16,128]{2,1,0:T(8,128)S(1)} %bitcast.37, f32[160,16,128]{2,0,1:T(8,128)} %get-tuple-element.109, f32[16,128]{1,0:T(8,128)S(1)} %bitcast.46, f32[160,16]{0,1:T(8,128)S(1)} %add_rsqrt_fusion), kind=kOutput, calls=%fused_computation.3 | convolution fusion | flops 1344143360 | bytes 11683840 | tf_op jit(solution)/shard_map/dot_general | solution.py:53
  (31 shorter events, 17.3 us)
Async XLA Ops:
  6.5 1.6 copy-start.3
  6.5 199.9 %all-gather.6.cloned.1.call-start = ((), (), s32[]{:S(2)}) async-start(), calls=%async_computation.1 | async-start | bytes 34603008 | tf_op jit(solution)/shard_map/all_gather | solution.py:12
  8.3 0.9 copy-start
  10.7 288.9 %all-gather.4.cloned.1.call-start = ((), (), s32[]{:S(2)}) async-start(), calls=%async_computation | async-start | bytes 8912896 | tf_op jit(solution)/shard_map/all_gather | solution.py:55
  11.5 2.5 copy-start.2
  206.5 51.9 %copy-start.1 = (bf16[20,8,16,128]{3,2,1,0:T(8,128)(2,1)S(1)}, bf16[20,8,16,128]{3,2,1,0:T(8,128)(2,1)}, u32[]{:S(2)}) copy-start(bf16[20,8,16,128]{3,2,1,0:T(8,128)(2,1)} %copy.26) | copy-start | bytes 1966084
  258.4 41.2 %copy-start.4 = (f32[2048]{0:T(1024)S(1)}, f32[2048]{0:T(1024)}, u32[]{:S(2)}) copy-start(f32[2048]{0:T(1024)} %param.12) | copy-start | bytes 24580
Sparse Core Ops, SparseCore 0:
  10.8 195.6 all-gather.5
  209.5 90.0 all-gather.3
where the time goes:
time: 314 us; the launch traced here: 313 us
  waiting for transfers between devices  228 us (73%)
  other arithmetic  54.3 us (17%)
  matrix products  14.4 us (5%)
  between operations  13.5 us (4%)
    all_gather x1, waiting for transfers between devices, prefix_2(): everything = lax.all_gather(x, axis)  189 us
    select_n x32, other arithmetic, turn(): return jnp.where(reached, new, before)  51.1 us
    all_gather x1, waiting for transfers between devices, on_device(): lax.all_gather(out_weight, 'dp', axis=1, tiled=True)  38.1 us
    dot_general x1, matrix products, on_device(): jnp.dot(dropped, lax.all_gather(out_weight, 'dp', axis=1, tiled=True), pr...  6.56 us
  transfers between devices with their start and end apart: 2, of which 2 were waited for; matrix products, arithmetic and copies ran while one was open for 19% of the time, Pallas kernels for 0%

commit v1 on v0

--- a/solution.py
+++ b/solution.py
@@ -5,6 +5,9 @@
 
 HEADS = 16
 HEAD = 128
+connect_notes_in = lambda axis_name, panel: jnp.concatenate(
+    lax.all_to_all(jnp.stack([panel] * lax.axis_size(axis_name)), axis_name, 0, 0), axis=1
+)
 
 
 def prefix_2(x, axis, combine, identity):
@@ -51,9 +54,7 @@
     mask = keep[0].reshape(tok_rows, HEADS, HEAD).astype(jnp.float32)
     dropped = (normed * mask * (1.0 / 0.9)).astype(jnp.bfloat16).reshape(tok_rows, HEADS * HEAD)
     result = jnp.dot(
-        dropped,
-        lax.all_gather(out_weight, "dp", axis=1, tiled=True),
-        preferred_element_type=jnp.float32,
+        dropped, connect_notes_in("dp", out_weight), preferred_element_type=jnp.float32
     ).astype(jnp.bfloat16)
     return result[None]
 

time: 314 us -> 278 us (0.89)
  the two profiles are of different devices: /device:TPU:2 before, /device:TPU:1 now
where the time goes in v1:
time: 278 us; the launch traced here: 277 us
  waiting for transfers between devices  178 us (64%)
  other arithmetic  54.2 us (19%)
  matrix products  15.4 us (6%)
  between operations  13.5 us (5%)
  starting transfers between devices  7.76 us (3%)
  local copies, waits for them, and re-layouts  6.85 us (2%)
    all_gather x1, waiting for transfers between devices, prefix_2(): everything = lax.all_gather(x, axis)  178 us
    select_n x32, other arithmetic, turn(): return jnp.where(reached, new, before)  50.9 us
    all_to_all x1, starting transfers between devices, lax.all_to_all(jnp.stack([panel] * lax.axis_size(axis_name)), axis_name,...  7.76 us
    dot_general x1, matrix products, on_device(): jnp.dot(dropped, connect_notes_in('dp', out_weight), preferred_element_ty...  7.64 us
  transfers between devices with their start and end apart: 2, of which 1 were waited for; matrix products, arithmetic and copies ran while one was open for 23% of the time, Pallas kernels for 0%

profile of v1, /device:TPU:1, one launch (start us, length us, event | category | flops | bytes accessed | tf_op | source)
XLA Modules:
  0.0 277.0 jit_solution(3450503509679357759)
XLA Ops:
  10.9 4.3 %stack.2 = bf16[16,2048,128]{1,2,0:T(8,128)(2,1)} broadcast(bf16[2048,128]{0,1:T(8,128)(2,1)S(1)} %copy.26), dimensions={1,2} | broadcast | bytes 8912896 | tf_op jit(solution)/shard_map/stack | solution.py:9
  15.2 7.8 %all-to-all-start = ((bf16[16,2048,128]{1,2,0:T(8,128)(2,1)}), bf16[16,2048,128]{1,2,0:T(8,128)(2,1)}, u32[]{:S(2)}, u32[]{:S(2)}) async-start(bf16[16,2048,128]{1,2,0:T(8,128)(2,1)} %stack.2), calls=%async_computation | async-start | bytes 16777216 | tf_op jit(solution)/shard_map/all_to_all | solution.py:9
  26.0 3.3 %fusion.3 = f32[160,16,128]{2,0,1:T(8,128)} fusion(pred[160,160]{1,0:T(8,128)(4,1)S(1)} %iota_compare_fusion, bf16[160,16,128]{2,1,0:T(8,128)(2,1)} %bitcast.45, bf16[160,16,128]{2,1,0:T(8,128)(2,1)} %bitcast.44, bf16[160,16,128]{2,1,0:T(8,128)(2,1)S(1)} %bitcast.42), kind=kOutput, calls=%fused_computation.13 | convolution fusion | flops 210534400 | bytes 3302400 | tf_op jit(solution)/shard_map/hts,shd->thd/dot_general | solution.py:47
  29.3 178.4 %all-gather.3.cloned.1.call-done = f32[512,128,128]{2,1,0:T(8,128)} async-done(((f32[16,128,128]{2,1,0:T(8,128)}), f32[512,128,128]{2,1,0:T(8,128)}) %all-gather.3.cloned.1.call-update) | async-done | bytes 33554448 | tf_op jit(solution)/shard_map/all_gather | solution.py:15
  207.7 51.7 %while.14 = (s32[]{:T(128)}, f32[16,128,128]{2,1,0:T(8,128)S(1)}, s32[]{:T(128)}, f32[32,16,128,128]{3,2,1,0:T(8,128)}, s32[]{:T(128)}, /*index=5*/s32[]{:T(128)}) while((s32[]{:T(128)}, f32[16,128,128]{2,1,0:T(8,128)S(1)}, s32[]{:T(128)}, f32[32,16,128,128]{3,2,1,0:T(8,128)}, s32[]{:T(128)}, /*index=5*/s32[]{:T(128)}) %tuple.38), condition=%wide.region_1.2_spmd.clone, body=%wide.region_0.1_spmd.clone.sunk | while | flops 786436 | bytes 3145821 | solution.py:23
  207.7 1.7 add_select_fusion.2
  209.4 1.6 add_select_fusion.2
  211.0 1.6 add_select_fusion.2
  212.6 1.6 add_select_fusion.2
  214.2 1.6 add_select_fusion.2
  215.8 1.6 add_select_fusion.2
  217.5 1.6 add_select_fusion.2
  219.1 1.6 add_select_fusion.2
  220.7 1.6 add_select_fusion.2
  222.3 1.6 add_select_fusion.2
  223.9 1.6 add_select_fusion.2
  225.5 1.6 add_select_fusion.2
  230.4 1.6 add_select_fusion.2
  232.0 1.6 add_select_fusion.2
  233.6 1.6 add_select_fusion.2
  236.8 1.6 add_select_fusion.2
  238.4 1.6 add_select_fusion.2
  240.0 1.6 add_select_fusion.2
  241.7 1.6 add_select_fusion.2
  244.9 1.6 add_select_fusion.2
  246.5 1.6 add_select_fusion.2
  248.1 1.6 add_select_fusion.2
  253.0 1.6 add_select_fusion.2
  254.6 1.6 add_select_fusion.2
  256.2 1.6 add_select_fusion.2
  259.4 3.0 %multiply_reduce_fusion = (f32[160,16]{0,1:T(8,128)S(1)}, f32[160,16,128]{2,0,1:T(8,128)}) fusion(f32[160,16,128]{2,0,1:T(8,128)} %fusion.3, f32[16,128,128]{2,1,0:T(8,128)S(1)} %get-tuple-element.84, bf16[160,16,128]{2,1,0:T(8,128)(2,1)S(1)} %bitcast.46), kind=kOutput, calls=%fused_computation.24 | convolution fusion | flops 85128704 | bytes 4335616 | tf_op jit(solution)/shard_map/thc,hcd->thd/dot_general | solution.py:43
  262.5 7.6 %fusion = bf16[1,160,2048]{2,1,0:T(8,128)(2,1)} fusion(bf16[2048,2048]{0,1:T(8,128)(2,1)} %bitcast.5, f32[160,16,128]{2,1,0:T(8,128)S(1)} %bitcast.40, f32[160,16,128]{2,0,1:T(8,128)} %get-tuple-element.109, f32[16,128]{1,0:T(8,128)S(1)} %bitcast.49, f32[160,16]{0,1:T(8,128)S(1)} %add_rsqrt_fusion), kind=kOutput, calls=%fused_computation.3 | convolution fusion | flops 1344143360 | bytes 11683840 | tf_op jit(solution)/shard_map/dot_general | solution.py:56
  (34 shorter events, 18.4 us)
Async XLA Ops:
  6.5 1.6 copy-start.2
  6.5 201.2 %all-gather.3.cloned.1.call-start = ((), (), s32[]{:S(2)}) async-start(), calls=%async_computation.1 | async-start | bytes 34603008 | tf_op jit(solution)/shard_map/all_gather | solution.py:15
  8.3 0.8 copy-start
  9.2 1.5 copy-start.4
  15.2 7.8 %copy-start.3 = (bf16[1,160,2048]{2,1,0:T(8,128)(2,1)S(1)}, bf16[1,160,2048]{2,1,0:T(8,128)(2,1)}, u32[]{:S(2)}) copy-start(bf16[1,160,2048]{2,1,0:T(8,128)(2,1)} %param.8) | copy-start | bytes 1966084
  15.2 247.2 %all-to-all-start = ((bf16[16,2048,128]{1,2,0:T(8,128)(2,1)}), bf16[16,2048,128]{1,2,0:T(8,128)(2,1)}, u32[]{:S(2)}, u32[]{:S(2)}) async-start(bf16[16,2048,128]{1,2,0:T(8,128)(2,1)} %stack.2), calls=%async_computation | async-start | bytes 16777216 | tf_op jit(solution)/shard_map/all_to_all | solution.py:9
  207.7 51.7 %copy-start.1 = (bf16[20,8,16,128]{3,2,1,0:T(8,128)(2,1)S(1)}, bf16[20,8,16,128]{3,2,1,0:T(8,128)(2,1)}, u32[]{:S(2)}) copy-start(bf16[20,8,16,128]{3,2,1,0:T(8,128)(2,1)} %copy.28) | copy-start | bytes 1966084
  259.4 3.1 %copy-start.5 = (f32[2048]{0:T(1024)S(1)}, f32[2048]{0:T(1024)}, u32[]{:S(2)}) copy-start(f32[2048]{0:T(1024)} %param.12) | copy-start | bytes 24580
Sparse Core Ops, SparseCore 0:
  10.8 196.8 all-gather.2
